TPU v7x, 128 devices: a whole 4x4x4 slice. The times are simulated.
128 devices in a mesh: dp: 8 (over x_lo, z), param: 16 (over x_hi, y, core).
Axes of the slice: x: 4 (x_hi: 2, x_lo: 2; x = x_hi * 2 + x_lo), y: 4, z: 4, core: 2. Of those that a mesh axis runs over, the one named last changes fastest.
Arguments:
- train_grads: bfloat16 [512, 262144], P('dp', 'param'), may hold values from -6 to 6
- target_grads: bfloat16 [256, 262144], P('dp', 'param'), may hold values from -6 to 6
- projection: bfloat16 [1024, 262144], P('dp', 'param'), may hold values from -0.01171875 to 0.01171875
- first_moment: float32 [16, 8, 2048], P('param', 'dp'), may hold values from -0.3 to 0.3
- second_moment: float32 [16, 8, 2048], P('param', 'dp'), may hold values from 0.001 to 0.1
- owner_map: int32 [16, 8], P('param'), may hold values from 0 to 7, as said below
Outputs:
- similarity: float32 [512, 256], P(('dp', 'param'))
Inputs may be any that keep to these rules, and one draw needn't show every extreme that they name: `owner_map`: each row is a permutation of 0 to 7.
All inputs are finite; a program needn't handle non-finite values.
Results may differ from a plain program's by a relative error of at most 0.0029.
Values may be sent and summed in bfloat16 or wider, within the bound.
A program may use at most 128 MiB of HBM per device.

v0:
```python
import math

import jax
import jax.numpy as jnp
from jax import lax
from jax.sharding import PartitionSpec as P


def side_by_side(arrays, axis, dim, along):
    both = jnp.concatenate(arrays, axis=along)
    filled, at, done = (lax.all_gather(both, axis, axis=dim, tiled=True), 0, [])
    for a in arrays:
        done.append(lax.slice_in_dim(filled, at, at + a.shape[along], axis=along))
        at += a.shape[along]
    return tuple(done)


def split_up(value, dim, length):
    shape = value.shape
    blocks = value.reshape(*shape[:dim], length, shape[dim] // length, *shape[dim + 1 :])
    return jnp.moveaxis(blocks, dim, 0)


def summed_on_arrival(value, axis, dim):
    blocks = split_up(value, dim, lax.axis_size(axis))
    arrived = lax.all_to_all(blocks, axis, split_axis=0, concat_axis=0, tiled=True)
    return arrived.sum(axis=0)


def precondition(grad_rows, first_full, second_full):
    grad_f32 = grad_rows.astype(jnp.float32)
    upper = 0.9 * first_full + 0.1 * grad_f32
    lower = jnp.sqrt(0.999 * second_full + 0.001 * grad_f32 * grad_f32) + 1e-08
    return (upper / lower).astype(jnp.bfloat16)


def project(grad_rows, projection):
    return lax.dot_general(
        grad_rows, projection, (((1,), (1,)), ((), ())), preferred_element_type=jnp.float32
    )


def per_device(train_grads, target_grads, projection, first_moment, second_moment, owner_map):
    dp_count = lax.axis_size("dp")
    param_count = lax.axis_size("param")
    first_all, second_all = side_by_side((first_moment, second_moment), "dp", 1, 0)
    first_full = jnp.take(first_all[0], owner_map[0], axis=0).reshape(-1)
    second_full = jnp.take(second_all[0], owner_map[0], axis=0).reshape(-1)
    updates = precondition(train_grads, first_full, second_full)
    train_rows = updates.shape[0]
    target_rows = target_grads.shape[0]
    own_train = train_rows // param_count
    own_target = target_rows // param_count
    stacked = jnp.concatenate((updates, target_grads), axis=0)
    partial_value = project(lax.all_gather(stacked, "dp", axis=0, tiled=True), projection)
    feature_cols = partial_value.shape[1]
    partial_value = partial_value.reshape(dp_count, train_rows + target_rows, feature_cols)
    train_part = partial_value[:, :train_rows].reshape(
        dp_count, param_count, own_train, feature_cols
    )
    target_part = partial_value[:, train_rows:].reshape(
        dp_count, param_count, own_target, feature_cols
    )
    blocks = jnp.concatenate((train_part, target_part), axis=2).transpose(1, 0, 2, 3)
    summed = summed_on_arrival(blocks, "param", 0)
    regrouped = lax.all_to_all(summed, "dp", split_axis=1, concat_axis=3, tiled=True)
    features = regrouped.reshape(own_train + own_target, -1)
    unit_rows = features * lax.rsqrt(jnp.mean(features * features, axis=1, keepdims=True) + 1e-06)
    everyone = lax.all_gather(unit_rows[own_train:], ("dp", "param"), axis=0, tiled=True)
    similarity = jnp.dot(
        unit_rows[:own_train],
        everyone.T,
        precision=lax.Precision.HIGHEST,
        preferred_element_type=jnp.float32,
    )
    return similarity / math.sqrt(unit_rows.shape[1])


def solution(mesh):
    placed = (
        P("dp", "param"),
        P("dp", "param"),
        P("dp", "param"),
        P("param", "dp", None),
        P("param", "dp", None),
        P("param", None),
    )
    return jax.shard_map(
        per_device, mesh=mesh, in_specs=placed, out_specs=P(("dp", "param"), None), check_vma=False
    )
```

profile of v0, /device:TPU:0, one launch (start us, length us, event | category | flops | bytes accessed | tf_op | source)
XLA Modules:
  0.0 537.2 jit_solution(719248493598214134)
XLA Ops:
  6.5 0.7 compare_and_fusion
  7.3 0.7 compare_select_fusion
  8.0 0.7 pad_maximum_fusion.1
  8.7 29.5 %all_gather.9 = f32[2,8,2048]{2,0,1:T(2,128)S(1)} all-gather(f32[2,1,2048]{2,0,1:T(2,128)S(1)} %pad_maximum_fusion.1), channel_id=1, replica_groups=mesh['dp'=8,'param'=16] {'dp'}, dimensions={1}, use_global_device_ids=true | all-gather | bytes 147456 | tf_op jit(solution)/shard_map/all_gather | solution.py:11
  38.2 0.1 fusion.9
  38.4 0.6 gather_fusion.1
  38.9 0.6 gather_fusion
  39.5 0.1 fusion.7
  39.7 3.8 fusion.2
  43.5 1.9 pad_maximum_fusion
  45.4 0.0 all-gather.4.cloned.1.call-update
  45.5 0.0 all-gather.6.cloned.1.call-start
  45.5 250.6 %all-gather.4.cloned.1.call-done = bf16[768,16384]{1,0:T(8,128)(2,1)} async-done(((bf16[96,16384]{1,0:T(8,128)(2,1)}), bf16[768,16384]{1,0:T(8,128)(2,1)}) %all-gather.4.cloned.1.call-update) | async-done | bytes 25165840 | tf_op jit(solution)/shard_map/all_gather | solution.py:55
  296.2 12.8 %fusion.10 = f32[768,128]{1,0:T(8,128)S(1)} fusion(bf16[768,16384]{1,0:T(8,128)(2,1)} %all-gather.4.cloned.1.call-done, bf16[128,16384]{1,0:T(8,128)(2,1)} %param.10), kind=kOutput, calls=%fused_computation.30 | convolution fusion | flops 3221225472 | bytes 29753344 | tf_op jit(solution)/shard_map/dot_general | solution.py:38
  309.0 0.2 copy.17
  309.2 0.1 copy.18
  309.3 17.2 %all_to_all.20 = f32[16,1,8,6,128]{4,2,3,1,0:T(8,128)S(1)} all-to-all(f32[16,1,8,6,128]{4,2,3,1,0:T(8,128)S(1)} %maximum_bitcast_fusion), channel_id=1, replica_groups=mesh['dp'=8,'param'=16] {'param'}, dimensions={0} | all-to-all | bytes 786432 | tf_op jit(solution)/shard_map/all_to_all | solution.py:26
  326.6 8.6 %all_to_all.21 = f32[1,8,6,128]{3,0,2,1:T(1,128)S(1)} all-to-all(f32[1,8,6,128]{3,0,2,1:T(1,128)S(1)} %copy.19), channel_id=1, replica_groups=mesh['dp'=8,'param'=16] {'dp'}, dimensions={1} | all-to-all | bytes 49152 | tf_op jit(solution)/shard_map/all_to_all | solution.py:66
  335.2 0.1 multiply_reduce_fusion
  335.3 0.1 bitcast_multiply_fusion
  335.4 0.6 slice_bitcast_fusion
  336.1 190.9 %all-gather.6.cloned.1.call-done = f32[128,2,1024]{2,1,0:T(2,128)} async-done(((f32[1,2,1024]{2,1,0:T(2,128)}), f32[128,2,1024]{2,1,0:T(2,128)}) %all-gather.6.cloned.1.call-update) | async-done | bytes 1048592 | tf_op jit(solution)/shard_map/all_gather | solution.py:69
  526.9 1.9 reshape.70
  528.9 1.5 convolution_multiply_fusion
  (15 shorter events, 0.2 us)
Async XLA Ops:
  6.5 37.0 %copy-start = (bf16[32,16384]{1,0:T(8,128)(2,1)S(1)}, bf16[32,16384]{1,0:T(8,128)(2,1)}, u32[]{:S(2)}) copy-start(bf16[32,16384]{1,0:T(8,128)(2,1)} %param.9) | copy-start | bytes 3145732
  6.5 289.6 %all-gather.4.cloned.1.call-start = ((), (), s32[]{:S(2)}) async-start(), calls=%async_computation.2 | async-start | bytes 28311552 | tf_op jit(solution)/shard_map/all_gather | solution.py:55
  45.5 481.5 %all-gather.6.cloned.1.call-start = ((), (), s32[]{:S(2)}) async-start(), calls=%async_computation.3 | async-start | bytes 1056768 | tf_op jit(solution)/shard_map/all_gather | solution.py:69
Sparse Core Ops, SparseCore 0:
  45.6 250.5 all-gather.3
  336.2 190.7 all-gather.5
where the time goes:
time: 538 us; the launch traced here: 537 us
  waiting for transfers between devices  442 us (82%)
  blocking collectives  55.4 us (10%)
  matrix products  14.3 us (3%)
  between operations  13.5 us (3%)
  other arithmetic  8.29 us (2%)
    all_gather x1, waiting for transfers between devices, per_device(): lax.all_gather(stacked, 'dp', axis=0, tiled=True)  251 us
    all_gather x1, waiting for transfers between devices, per_device(): lax.all_gather(unit_rows[own_train:], ('dp', 'param'), axis=0, tiled=True)  191 us
    all_gather x1, blocking collectives, side_by_side(): filled, at, done = (lax.all_gather(both, axis, axis=dim, tiled=True), 0, [])  29.5 us
    all_to_all x1, blocking collectives, summed_on_arrival(): lax.all_to_all(blocks, axis, split_axis=0, concat_axis=0, tiled=True)  17.2 us
    dot_general x1, matrix products, project(): lax.dot_general(grad_rows, projection, (((1,), (1,)), ((), ())), preferre...  12.8 us
  transfers between devices with their start and end apart: 2, of which 2 were waited for; matrix products, arithmetic and copies ran while one was open for 0% of the time, Pallas kernels for 0%

commit v1 on v0

v1 whole, which is shorter than its diff:
```python
import functools
import math

import jax
import jax.numpy as jnp
from jax import lax
from jax.experimental import pallas as pl
from jax.experimental.pallas import tpu as pltpu
from jax.sharding import PartitionSpec as P

MESH = pl.DeviceIdType.MESH
F32, BF16 = jnp.float32, jnp.bfloat16
COLS = 2048
FEATS = 1024
GROUPS = 6
TGROUPS = 2


def one_hot(rows, source_of):
    r = lax.broadcasted_iota(jnp.int32, (rows, rows), 0)
    s = lax.broadcasted_iota(jnp.int32, (rows, rows), 1)
    return jnp.where(source_of(r) == s, 1.0, 0.0).astype(BF16)


def bits(r, low, width):
    return (r >> low) & ((1 << width) - 1)


def kernel(
    train, target, proj, first, second, owners,
    out,
    raw_rows, raw_targets, sorted_rows, sorted_targets,
    all_proj, all_rows, all_first, all_second, mixed, lhs,
    partial, from_core, by_y, from_y, by_xz, from_xz, unit, unit_cat, own_rows,
    load_sem, mom_sem, proj_sem, row_sem, core_sem, y_sem, xz_sem, unit_sem,
):
    dp = lax.axis_index("dp")
    param = lax.axis_index("param")
    x_hi, y, core = param // 8, (param // 2) % 4, param % 2
    place = x_hi * 8 + dp

    def dp_peer(o):
        return (dp + o) % 8, {"dp": (dp + o) % 8, "param": param}

    core_peer = {"dp": dp, "param": x_hi * 8 + y * 2 + (1 - core)}

    def y_peer(o):
        other = (y + o) % 4
        return other, {"dp": dp, "param": x_hi * 8 + other * 2 + core}

    def xz_peer(o):
        far, near = (x_hi + o // 8) % 2, (dp + o % 8) % 8
        return far * 8 + near, {"dp": near, "param": far * 8 + y * 2 + core}

    def send(src, dst, sems, at, device):
        pltpu.make_async_remote_copy(
            src_ref=src, dst_ref=dst, send_sem=sems.at[0, at], recv_sem=sems.at[1, at],
            device_id=device, device_id_type=MESH,
        ).start()

    def keep(src, dst, sem):
        pltpu.make_async_copy(src, dst, sem).start()

    def wait(ref, sem):
        pltpu.make_async_copy(ref, ref, sem).wait()

    keep(target, raw_targets, load_sem.at[0])
    keep(train, raw_rows, load_sem.at[1])
    barrier = pltpu.get_barrier_semaphore()
    peers = [xz_peer(o)[1] for o in range(1, 16)] + [core_peer] + [y_peer(o)[1] for o in range(1, 4)]
    for device in peers:
        pl.semaphore_signal(barrier, inc=1, device_id=device, device_id_type=MESH)
    pl.semaphore_wait(barrier, len(peers))

    keep(first.at[0], all_first.at[dp], mom_sem.at[1, 0])
    keep(second.at[0], all_second.at[dp], mom_sem.at[1, 1])
    order = (2, 6, 5, 7, 1, 3, 4)
    for o in order:
        other, device = dp_peer(o)
        send(first.at[0], all_first.at[dp], mom_sem, 0, device)
        send(second.at[0], all_second.at[dp], mom_sem, 1, device)
    for o in order:
        other, device = dp_peer(o)
        send(proj.at[:, pl.ds(other * COLS, COLS)], all_proj.at[dp], proj_sem, 0, device)
    keep(proj.at[:, pl.ds(dp * COLS, COLS)], all_proj.at[dp], proj_sem.at[1, 0])

    def sort(raw, done, groups):
        rows = groups * 16
        pick = one_hot(rows, lambda r: (r & 15) * groups + (r >> 4))

        @pl.loop(0, 16)
        def _(t):
            cols = pl.ds(pl.multiple_of(t * 1024, 1024), 1024)
            done[:, cols] = jnp.dot(pick, raw[:, cols], preferred_element_type=F32).astype(BF16)

    def send_rows(k):
        done, at = (sorted_targets, k) if k < TGROUPS else (sorted_rows, k - TGROUPS)
        rows = pl.ds(at * 16, 16)
        for o in order:
            other, device = dp_peer(o)
            send(done.at[rows, pl.ds(other * COLS, COLS)], all_rows.at[k, dp], row_sem, k, device)
        keep(done.at[rows, pl.ds(dp * COLS, COLS)], all_rows.at[k, dp], row_sem.at[1, k])

    wait(raw_targets, load_sem.at[0])
    sort(raw_targets, sorted_targets, 2)
    wait(raw_rows, load_sem.at[1])
    sort(raw_rows, sorted_rows, 4)
    for k in range(GROUPS):
        send_rows(k)

    wait(all_first, mom_sem.at[1, 0])
    wait(all_second, mom_sem.at[1, 1])
    owner = owners[0, dp]
    first_row = 0.9 * all_first[owner]
    second_row = 0.999 * all_second[owner]

    regroup = one_hot(
        128, lambda r: bits(r, 0, 3) * 16 + bits(r, 3, 1) * 8 + bits(r, 4, 2) * 2 + bits(r, 6, 1)
    )

    def multiply(k):
        wait(all_rows.at[k], row_sem.at[1, k])
        if k >= TGROUPS:

            @pl.loop(0, 8)
            def _(s):
                for t in range(4):
                    cols = slice(t * 512, (t + 1) * 512)
                    g = all_rows[k, s, :, cols].astype(F32)
                    upper = first_row[:, cols] + 0.1 * g
                    lower = jnp.sqrt(second_row[:, cols] + 0.001 * g * g) + 1e-08
                    mixed[s, :, cols] = (upper / lower).astype(BF16)

        @pl.loop(0, 4)
        def _(t):
            cols = pl.ds(pl.multiple_of(t * 512, 512), 512)
            rows = mixed[:, :, cols] if k >= TGROUPS else all_rows[k, :, :, cols]
            lhs[:, cols] = jnp.dot(
                regroup, rows.reshape(128, 512), preferred_element_type=F32
            ).astype(BF16)

        @pl.loop(0, 4)
        def _(t):
            some = all_proj[pl.ds(t * 2, 2)].reshape(256, COLS)
            partial[k, :, pl.ds(pl.multiple_of(t * 256, 256), 256)] = lax.dot_general(
                lhs[...], some, (((1,), (1,)), ((), ())), preferred_element_type=F32
            )

        send(partial.at[k, pl.ds((1 - core) * 64, 64)], from_core.at[k], core_sem, k, core_peer)

    def add_core(k):
        wait(from_core.at[k], core_sem.at[1, k])

        @pl.loop(0, 4)
        def _(t):
            rows = pl.ds(t * 16, 16)
            by_y[k, rows] = partial[k, pl.ds(core * 64 + t * 16, 16)] + from_core[k, rows]

        for o in (2, 1, 3):
            other, device = y_peer(o)
            send(by_y.at[k, pl.ds(other * 16, 16)], from_y.at[k, o - 1], y_sem, k, device)

    def add_y(k):
        wait(from_y.at[k], y_sem.at[1, k])
        total = by_y[k, pl.ds(y * 16, 16)] + from_y[k, 0] + from_y[k, 1] + from_y[k, 2]
        for s in range(8):
            by_xz[k, pl.ds(s, 16, stride=8), :] = total[:, s * 128 : (s + 1) * 128]
        for o in range(1, 16):
            other, device = xz_peer(o)
            send(by_xz.at[k, pl.ds(other * 8, 8)], from_xz.at[k, pl.ds(o * 8 - 8, 8)], xz_sem, k, device)

    def unit_row(k):
        wait(from_xz.at[k], xz_sem.at[1, k])
        f = by_xz[k, pl.ds(place * 8, 8)]
        for o in range(15):
            f = f + from_xz[k, o * 8 : o * 8 + 8]
        mean = jnp.sum(f * f, keepdims=True) / FEATS
        return f * lax.rsqrt(mean + 1e-06)

    spot = (core * 4 + y) * 16 + place

    def target_row(k):
        unit[pl.ds(spot * 16 + k * 8, 8)] = unit_row(k)

    def train_row(k):
        own_rows[(k - TGROUPS) * 8 : (k - TGROUPS + 1) * 8] = unit_row(k)

    def gather_xz():
        mine = unit.at[pl.ds(spot * 16, 16)]
        for o in range(1, 16):
            send(mine, mine, unit_sem, 0, xz_peer(o)[1])

    def gather_y():
        wait(unit.at[pl.ds(0, 240)], unit_sem.at[1, 0])
        mine = unit.at[pl.ds((core * 4 + y) * 256, 256)]
        for o in (2, 1, 3):
            send(mine, mine, unit_sem, 1, y_peer(o)[1])

    def gather_core():
        wait(unit.at[pl.ds(0, 768)], unit_sem.at[1, 1])
        mine = unit.at[pl.ds(core * 1024, 1024)]
        send(mine, mine, unit_sem, 2, core_peer)

    def arrange():
        wait(unit.at[pl.ds(0, 1024)], unit_sem.at[1, 2])
        natural = one_hot(
            256,
            lambda r: bits(r, 1, 1) * 128 + bits(r, 2, 2) * 32 + bits(r, 4, 1) * 16
            + bits(r, 5, 3) * 2 + bits(r, 0, 1),
        )
        for s in range(8):
            piece = unit[pl.ds(s, 256, stride=8), :]
            high = piece.astype(BF16)
            low = (piece - high.astype(F32)).astype(BF16)
            cols = slice(s * 128, (s + 1) * 128)
            unit_cat[0:256, cols] = jnp.dot(natural, high, preferred_element_type=F32).astype(BF16)
            unit_cat[256:512, cols] = jnp.dot(natural, low, preferred_element_type=F32).astype(BF16)

    wait(all_proj, proj_sem.at[1, 0])
    own_rows[...] = jnp.zeros_like(own_rows)
    multiply(0)
    multiply(1)
    add_core(0)
    add_core(1)
    multiply(2)
    add_y(0)
    add_y(1)
    add_core(2)
    multiply(3)
    target_row(0)
    target_row(1)
    gather_xz()
    add_y(2)
    add_core(3)
    multiply(4)
    gather_y()
    train_row(2)
    add_y(3)
    add_core(4)
    multiply(5)
    gather_core()
    train_row(3)
    add_y(4)
    add_core(5)
    arrange()
    train_row(4)
    add_y(5)
    train_row(5)

    rows = jnp.concatenate([own_rows[pl.ds(s, 8, stride=8), :] for s in range(8)], axis=1)
    high = rows.astype(BF16)
    low = (rows - high.astype(F32)).astype(BF16)
    product = lax.dot_general(
        jnp.concatenate([high, low], axis=0), unit_cat[...], (((1,), (1,)), ((), ())),
        preferred_element_type=F32,
    )
    scaled = product[0:8, 0:256] + (product[8:16, 0:256] + product[0:8, 256:512])
    out[...] = scaled[0:4] / math.sqrt(FEATS)

    wait(all_first.at[pl.ds(0, 7)], mom_sem.at[0, 0])
    wait(all_second.at[pl.ds(0, 7)], mom_sem.at[0, 1])
    wait(all_proj.at[pl.ds(0, 7)], proj_sem.at[0, 0])
    for k in range(GROUPS):
        wait(all_rows.at[k, pl.ds(0, 7)], row_sem.at[0, k])
        wait(from_core.at[k], core_sem.at[0, k])
        wait(from_y.at[k], y_sem.at[0, k])
        wait(from_xz.at[k], xz_sem.at[0, k])
    wait(unit.at[pl.ds(0, 240)], unit_sem.at[0, 0])
    wait(unit.at[pl.ds(0, 768)], unit_sem.at[0, 1])
    wait(unit.at[pl.ds(0, 1024)], unit_sem.at[0, 2])


def per_device(train, target, proj, first, second, owners):
    vmem = pltpu.VMEM
    dma = pltpu.SemaphoreType.DMA
    anywhere = pl.BlockSpec(memory_space=pl.ANY)
    return pl.pallas_call(
        kernel,
        out_shape=jax.ShapeDtypeStruct((4, 256), F32),
        in_specs=[anywhere] * 5 + [pl.BlockSpec(memory_space=pltpu.SMEM)],
        out_specs=pl.BlockSpec(memory_space=pltpu.VMEM),
        scratch_shapes=[
            vmem((64, 16384), BF16),
            vmem((32, 16384), BF16),
            vmem((64, 16384), BF16),
            vmem((32, 16384), BF16),
            vmem((8, 128, COLS), BF16),
            vmem((GROUPS, 8, 16, COLS), BF16),
            vmem((8, 1, COLS), F32),
            vmem((8, 1, COLS), F32),
            vmem((8, 16, COLS), BF16),
            vmem((128, COLS), BF16),
            vmem((GROUPS, 128, FEATS), F32),
            vmem((GROUPS, 64, FEATS), F32),
            vmem((GROUPS, 64, FEATS), F32),
            vmem((GROUPS, 3, 16, FEATS), F32),
            vmem((GROUPS, 128, 128), F32),
            vmem((GROUPS, 120, 128), F32),
            vmem((2048, 128), F32),
            vmem((512, FEATS), BF16),
            vmem((64, 128), F32),
            dma((2,)),
            dma((2, 2)),
            dma((2, 1)),
            dma((2, GROUPS)),
            dma((2, GROUPS)),
            dma((2, GROUPS)),
            dma((2, GROUPS)),
            dma((2, 3)),
        ],
        compiler_params=pltpu.CompilerParams(
            collective_id=0, has_side_effects=True, vmem_limit_bytes=60 * 2**20
        ),
    )(train, target, proj, first, second, owners)


def solution(mesh):
    placed = (
        P("dp", "param"),
        P("dp", "param"),
        P("dp", "param"),
        P("param", "dp", None),
        P("param", "dp", None),
        P("param", None),
    )
    return jax.shard_map(
        per_device, mesh=mesh, in_specs=placed, out_specs=P(("dp", "param"), None), check_vma=False
    )
```

time: 538 us -> 122 us (0.23)
  waiting for transfers between devices: 442 us -> 0 us
  Pallas kernels: 0 us -> 121 us
  blocking collectives: 55.4 us -> 0 us
  matrix products: 14.3 us -> 0 us
  between operations: 13.5 us -> 0.01 us
  other arithmetic: 8.29 us -> 0 us
    all_gather x2 -> x0, waiting for transfers between devices: 442 us -> none  [the longest x1 251 us: per_device(): lax.all_gather(stacked, 'dp', axis=0, tiled=True)]
    pallas_call x0 -> x1, Pallas kernels: none -> 121 us  [per_device(): pl.pallas_call(kernel, out_shape=jax.ShapeDtypeStruct((4, 256), F32), in_...]
    all_gather x1 -> x0, blocking collectives: 29.5 us -> none  [side_by_side(): filled, at, done = (lax.all_gather(both, axis, axis=dim, tiled=True), 0, [])]
    all_to_all x2 -> x0, blocking collectives: 25.8 us -> none  [the longest x1 17.2 us: summed_on_arrival(): lax.all_to_all(blocks, axis, split_axis=0, concat_axis=0, tiled=True)]
    dot_general x2 -> x0, matrix products: 14.3 us -> none  [the longest x1 12.8 us: project(): lax.dot_general(grad_rows, projection, (((1,), (1,)), ((), ())), preferre...]
  transfers between devices with their start and end apart: 2 -> 0, of which waited for: 2 -> 0; matrix products, arithmetic and copies ran while one was open for 0% -> 0% of each run, Pallas kernels for 0% -> 0%
where the time goes in v1:
time: 122 us
  Pallas kernels  121 us (99%)
  local copies, waits for them, and re-layouts  1.28 us (1%)
    pallas_call x1, Pallas kernels, per_device(): pl.pallas_call(kernel, out_shape=jax.ShapeDtypeStruct((4, 256), F32), in_...  121 us

profile of v1, /device:TPU:0, one launch (start us, length us, event | category | flops | bytes accessed | tf_op | source)
XLA Modules:
  0.0 122.3 jit_solution(2063964324092435789)
XLA Ops:
  0.0 121.0 %shard_map.64 = f32[4,256]{1,0:T(4,128)} custom-call(bf16[64,16384]{1,0:T(8,128)(2,1)} %train.1, bf16[32,16384]{1,0:T(8,128)(2,1)} %target.1, bf16[128,16384]{1,0:T(8,128)(2,1)} %proj.1, f32[1,1,2048]{2,1,0:T(1,128)} %first.1, f32[1,1,2048]{2,1,0:T(1,128)} %second.1, s32[1,8]{1,0:T(1,128)} %owners.1), custom_call_target="tpu_custom_call" | custom-call | tf_op jit(solution)/shard_map/pallas_call | solution.py:277
  121.0 1.3 %copy.8 = f32[4,256]{1,0:T(4,128)} copy(f32[4,256]{1,0:T(4,128)} %shard_map.64) | data formatting | bytes 8192

commit v2 on v0

v2 whole, which is shorter than its diff:
```python
import math

import jax
import jax.numpy as jnp
from jax import lax
from jax.experimental import pallas as pl
from jax.experimental.pallas import tpu as pltpu
from jax.sharding import PartitionSpec as P

MESH = pl.DeviceIdType.MESH
F32, BF16 = jnp.float32, jnp.bfloat16
COLS = 2048
FEATS = 1024
HALF = 512
DEPTH = COLS // 2
PIECES = 8
GROUPS = 4
FAR_FIRST = (2, 6, 5, 7, 1, 3, 4)


def one_hot(rows, source_of, along=0):
    r = lax.broadcasted_iota(jnp.int32, (rows, rows), along)
    s = lax.broadcasted_iota(jnp.int32, (rows, rows), 1 - along)
    return jnp.where(source_of(r) == s, 1.0, 0.0).astype(BF16)


def bits(r, low, width):
    return (r >> low) & ((1 << width) - 1)


def kernel(
    train, target, proj, first, second, owners,
    out,
    raw_rows, sorted_rows, all_targets, all_proj, columns_of, all_rows, all_first, all_second,
    target_lhs, mixed, lhs,
    target_part, target_from_core, target_by_y, target_from_y,
    part, from_core, by_y, from_y, by_xz, from_xz, raw_unit, unit_cat, own_rows,
    load_sem, mom_sem, target_sem, proj_sem, row_sem, core_sem, y_sem, xz_sem, gather_sem,
):
    dp = lax.axis_index("dp")
    param = lax.axis_index("param")
    x_hi, y, core = param // 8, (param // 2) % 4, param % 2
    place = x_hi * 8 + dp

    def dp_peer(o):
        return (dp + o) % 8, {"dp": (dp + o) % 8, "param": param}

    core_peer = {"dp": dp, "param": x_hi * 8 + y * 2 + (1 - core)}

    def y_peer(o):
        other = (y + o) % 4
        return other, {"dp": dp, "param": x_hi * 8 + other * 2 + core}

    def xz_peer(o):
        far, near = (x_hi + o // 8) % 2, (dp + o % 8) % 8
        return far * 8 + near, {"dp": near, "param": far * 8 + y * 2 + core}

    def send(src, dst, sems, at, device):
        pltpu.make_async_remote_copy(
            src_ref=src, dst_ref=dst, send_sem=sems.at[0, at], recv_sem=sems.at[1, at],
            device_id=device, device_id_type=MESH,
        ).start()

    def keep(src, dst, sem):
        pltpu.make_async_copy(src, dst, sem).start()

    def wait(ref, sem):
        pltpu.make_async_copy(ref, ref, sem).wait()

    def columns(owner):
        return pl.ds(owner * COLS, COLS)

    keep(train, raw_rows, load_sem.at[0])
    barrier = pltpu.get_barrier_semaphore()
    peers = [xz_peer(o)[1] for o in range(1, 16)] + [core_peer] + [y_peer(o)[1] for o in range(1, 4)]
    for device in peers:
        pl.semaphore_signal(barrier, inc=1, device_id=device, device_id_type=MESH)
    pl.semaphore_wait(barrier, len(peers))

    def send_targets():
        for o in FAR_FIRST:
            other, device = dp_peer(o)
            send(target.at[:, columns(other)], all_targets.at[dp], target_sem, 0, device)
        keep(target.at[:, columns(dp)], all_targets.at[dp], target_sem.at[1, 0])

    def send_proj(i):
        rows = pl.ds(i * 16, 16)
        for o in FAR_FIRST:
            other, device = dp_peer(o)
            send(proj.at[rows, columns(other)], all_proj.at[i, dp], proj_sem, i, device)
        keep(proj.at[rows, columns(dp)], all_proj.at[i, dp], proj_sem.at[1, i])

    def send_moments():
        for o in FAR_FIRST:
            other, device = dp_peer(o)
            send(first.at[0], all_first.at[dp], mom_sem, 0, device)
            send(second.at[0], all_second.at[dp], mom_sem, 1, device)
        keep(first.at[0], all_first.at[dp], mom_sem.at[1, 0])
        keep(second.at[0], all_second.at[dp], mom_sem.at[1, 1])

    def send_rows(k, half):
        rows, at = pl.ds(k * 16, 16), k * 2 + half

        def some(owner):
            return sorted_rows.at[rows, pl.ds(owner * COLS + half * DEPTH, DEPTH)]

        for o in FAR_FIRST:
            other, device = dp_peer(o)
            send(some(other), all_rows.at[at, dp], row_sem, at, device)
        keep(some(dp), all_rows.at[at, dp], row_sem.at[1, at])

    def sort_rows():
        wait(raw_rows, load_sem.at[0])
        pick = one_hot(64, lambda r: (r & 15) * 4 + (r >> 4))

        @pl.loop(0, 16)
        def _(t):
            cols = pl.ds(pl.multiple_of(t * 1024, 1024), 1024)
            sorted_rows[:, cols] = jnp.dot(
                pick, raw_rows[:, cols], preferred_element_type=F32
            ).astype(BF16)

    def regroup_targets():
        wait(all_targets, target_sem.at[1, 0])
        regroup = one_hot(
            256,
            lambda r: bits(r, 1, 3) * 32 + bits(r, 4, 1) * 16 + bits(r, 5, 2) * 4
            + bits(r, 7, 1) * 2 + bits(r, 0, 1),
        )

        @pl.loop(0, 8)
        def _(t):
            cols = pl.ds(pl.multiple_of(t * 256, 256), 256)
            target_lhs[:, cols] = jnp.dot(
                regroup, all_targets[:, :, cols].reshape(256, 256), preferred_element_type=F32
            ).astype(BF16)

    def transpose(i):
        wait(all_proj.at[i], proj_sem.at[1, i])
        same = one_hot(256, lambda r: r)
        for t in range(8):
            at = slice(t * 256, (t + 1) * 256)
            columns_of[at, i * 128 : (i + 1) * 128] = lax.dot_general(
                same, all_proj[i, :, :, at].reshape(128, 256), (((1,), (1,)), ((), ())),
                preferred_element_type=F32,
            ).astype(BF16)

    def multiply_targets(h):
        target_part[h] = jnp.dot(
            target_lhs[...], columns_of[:, h * HALF : (h + 1) * HALF], preferred_element_type=F32
        )
        away = pl.ds((1 - core) * 128, 128)
        send(target_part.at[h, away], target_from_core.at[h], core_sem, h, core_peer)

    def multiply(k, half):
        at = k * 2 + half
        wait(all_rows.at[at], row_sem.at[1, at])

        @pl.loop(0, 8)
        def _(s):
            for t in range(2):
                cols = slice(t * 512, (t + 1) * 512)
                own = slice(half * DEPTH + t * 512, half * DEPTH + (t + 1) * 512)
                g = all_rows[at, s, :, cols].astype(F32)
                upper = first_row[:, own] + 0.1 * g
                lower = jnp.sqrt(second_row[:, own] + 0.001 * g * g) + 1e-08
                mixed[s, :, cols] = (upper / lower).astype(BF16)

        for t in range(2):
            cols = slice(t * 512, (t + 1) * 512)
            lhs[:, cols] = jnp.dot(
                regroup, mixed[:, :, cols].reshape(128, 512), preferred_element_type=F32
            ).astype(BF16)
        done = jnp.dot(
            lhs[...], columns_of[half * DEPTH : (half + 1) * DEPTH], preferred_element_type=F32
        )
        if half == 0:
            part[k] = done
        else:
            part[k] = part[k] + done
            away = pl.ds((1 - core) * 64, 64)
            send(part.at[k, away], from_core.at[k], core_sem, 2 + k, core_peer)

    def add_core(g):
        if g < 2:
            here, there, total, arrived, k, rows = (
                target_part, target_from_core, target_by_y, target_from_y, g, 32,
            )
        else:
            here, there, total, arrived, k, rows = part, from_core, by_y, from_y, g - 2, 16
        wait(there.at[k], core_sem.at[1, g])

        @pl.loop(0, 4)
        def _(t):
            at = pl.ds(t * rows, rows)
            total[k, at] = here[k, pl.ds((core * 4 + t) * rows, rows)] + there[k, at]

        for o in (2, 1, 3):
            other, device = y_peer(o)
            send(total.at[k, pl.ds(other * rows, rows)], arrived.at[k, o - 1], y_sem, g, device)

    def add_y(g):
        if g < 2:
            total, arrived, k, rows = target_by_y, target_from_y, g, 32
        else:
            total, arrived, k, rows = by_y, from_y, g - 2, 16
        wait(arrived.at[k], y_sem.at[1, g])
        done = total[k, pl.ds(y * rows, rows)] + arrived[k, 0] + arrived[k, 1] + arrived[k, 2]
        tiles = 128 // rows
        for s in range(tiles):
            by_xz[g, pl.ds(s, rows, stride=tiles), :] = done[:, s * 128 : (s + 1) * 128]
        for o in range(1, 16):
            other, device = xz_peer(o)
            send(by_xz.at[g, pl.ds(other * 8, 8)], from_xz.at[g, pl.ds(o * 8 - 8, 8)], xz_sem, g, device)

    def add_xz(g):
        wait(from_xz.at[g], xz_sem.at[1, g])
        f = by_xz[g, pl.ds(place * 8, 8)]
        for o in range(15):
            f = f + from_xz[g, o * 8 : o * 8 + 8]
        return f

    spot = (core * 4 + y) * 16 + place

    def gather_xz(h):
        mine = raw_unit.at[h, pl.ds(spot * 8, 8)]
        raw_unit[h, pl.ds(spot * 8, 8)] = add_xz(h)
        for o in range(1, 16):
            send(mine, mine, gather_sem, h * 3, xz_peer(o)[1])

    def gather_y(h):
        wait(raw_unit.at[h, pl.ds(0, 120)], gather_sem.at[1, h * 3])
        mine = raw_unit.at[h, pl.ds((core * 4 + y) * 128, 128)]
        for o in (2, 1, 3):
            send(mine, mine, gather_sem, h * 3 + 1, y_peer(o)[1])

    def gather_core(h):
        wait(raw_unit.at[h, pl.ds(0, 384)], gather_sem.at[1, h * 3 + 1])
        mine = raw_unit.at[h, pl.ds(core * 512, 512)]
        send(mine, mine, gather_sem, h * 3 + 2, core_peer)

    def arrange():
        for h in range(2):
            wait(raw_unit.at[h, pl.ds(0, 512)], gather_sem.at[1, h * 3 + 2])
        natural = one_hot(
            256,
            lambda r: bits(r, 0, 1) * 128 + bits(r, 1, 1) * 64 + bits(r, 2, 2) * 16
            + bits(r, 4, 1) * 8 + bits(r, 5, 3),
            along=1,
        )

        def piece(h, s, c):
            return raw_unit[h, pl.ds(c * 4 + s, 128, stride=8), :]

        scale = []
        for c in range(2):
            squares = jnp.zeros((128, 128), F32)
            for h in range(2):
                for s in range(4):
                    f = piece(h, s, c)
                    squares = squares + f * f
            mean = jnp.sum(squares, axis=1, keepdims=True) / FEATS
            scale.append(lax.rsqrt(mean + 1e-06))
        for h in range(2):
            for s in range(4):
                f = jnp.concatenate([(piece(h, s, c) * scale[c]).T for c in range(2)], axis=1)
                high = f.astype(BF16)
                low = (f - high.astype(F32)).astype(BF16)
                at = slice(h * HALF + s * 128, h * HALF + (s + 1) * 128)
                unit_cat[at, 0:256] = jnp.dot(high, natural, preferred_element_type=F32).astype(BF16)
                unit_cat[at, 256:512] = jnp.dot(low, natural, preferred_element_type=F32).astype(BF16)

    def train_row(g):
        f = add_xz(g)
        mean = jnp.sum(f * f, keepdims=True) / FEATS
        own_rows[(g - 2) * 8 : (g - 1) * 8] = f * lax.rsqrt(mean + 1e-06)

    send_targets()
    send_proj(0)
    send_moments()
    send_proj(1)
    own_rows[...] = jnp.zeros_like(own_rows)
    sort_rows()
    regroup_targets()
    send_proj(2)
    transpose(0)
    send_proj(3)
    transpose(1)
    send_proj(4)
    wait(all_first, mom_sem.at[1, 0])
    wait(all_second, mom_sem.at[1, 1])
    owner = owners[0, dp]
    first_row = 0.9 * all_first[owner]
    second_row = 0.999 * all_second[owner]
    regroup = one_hot(
        128, lambda r: bits(r, 0, 3) * 16 + bits(r, 3, 1) * 8 + bits(r, 4, 2) * 2 + bits(r, 6, 1)
    )

    transpose(2)
    send_proj(5)
    transpose(3)
    multiply_targets(0)
    send_proj(6)
    add_core(0)
    transpose(4)
    send_proj(7)
    transpose(5)
    add_y(0)
    send_rows(0, 0)
    send_rows(0, 1)
    transpose(6)
    send_rows(1, 0)
    transpose(7)
    multiply_targets(1)
    gather_xz(0)
    send_rows(1, 1)
    add_core(1)
    multiply(0, 0)
    multiply(0, 1)
    add_y(1)
    send_rows(2, 0)
    gather_y(0)
    send_rows(2, 1)
    add_core(2)
    multiply(1, 0)
    multiply(1, 1)
    gather_xz(1)
    send_rows(3, 0)
    send_rows(3, 1)
    add_core(3)
    add_y(2)
    gather_core(0)
    multiply(2, 0)
    multiply(2, 1)
    gather_y(1)
    add_y(3)
    add_core(4)
    multiply(3, 0)
    multiply(3, 1)
    gather_core(1)
    add_core(5)
    train_row(2)
    add_y(4)
    train_row(3)
    arrange()
    train_row(4)
    add_y(5)
    train_row(5)

    rows = jnp.concatenate([own_rows[pl.ds(s, 8, stride=8), :] for s in range(8)], axis=1)
    high = rows.astype(BF16)
    low = (rows - high.astype(F32)).astype(BF16)
    product = jnp.dot(
        jnp.concatenate([high, low], axis=0), unit_cat[...], preferred_element_type=F32
    )
    scaled = product[0:8, 0:256] + (product[8:16, 0:256] + product[0:8, 256:512])
    out[...] = scaled[0:4] / math.sqrt(FEATS)

    wait(all_targets.at[pl.ds(0, 7)], target_sem.at[0, 0])
    wait(all_first.at[pl.ds(0, 7)], mom_sem.at[0, 0])
    wait(all_second.at[pl.ds(0, 7)], mom_sem.at[0, 1])
    for i in range(PIECES):
        wait(all_proj.at[i, pl.ds(0, 7)], proj_sem.at[0, i])
    for h in range(2):
        wait(target_from_core.at[h], core_sem.at[0, h])
        wait(target_from_y.at[h], y_sem.at[0, h])
        wait(from_xz.at[h], xz_sem.at[0, h])
        wait(raw_unit.at[h, pl.ds(0, 120)], gather_sem.at[0, h * 3])
        wait(raw_unit.at[h, pl.ds(0, 384)], gather_sem.at[0, h * 3 + 1])
        wait(raw_unit.at[h, pl.ds(0, 512)], gather_sem.at[0, h * 3 + 2])
    for at in range(GROUPS * 2):
        wait(all_rows.at[at, pl.ds(0, 7)], row_sem.at[0, at])
    for k in range(GROUPS):
        wait(from_core.at[k], core_sem.at[0, 2 + k])
        wait(from_y.at[k], y_sem.at[0, 2 + k])
        wait(from_xz.at[2 + k], xz_sem.at[0, 2 + k])


def per_device(train, target, proj, first, second, owners):
    vmem = pltpu.VMEM
    dma = pltpu.SemaphoreType.DMA
    anywhere = pl.BlockSpec(memory_space=pl.ANY)
    return pl.pallas_call(
        kernel,
        out_shape=jax.ShapeDtypeStruct((4, 256), F32),
        in_specs=[anywhere] * 5 + [pl.BlockSpec(memory_space=pltpu.SMEM)],
        out_specs=pl.BlockSpec(memory_space=pltpu.VMEM),
        scratch_shapes=[
            vmem((64, 16384), BF16),
            vmem((64, 16384), BF16),
            vmem((8, 32, COLS), BF16),
            vmem((PIECES, 8, 16, COLS), BF16),
            vmem((COLS, FEATS), BF16),
            vmem((GROUPS * 2, 8, 16, DEPTH), BF16),
            vmem((8, 1, COLS), F32),
            vmem((8, 1, COLS), F32),
            vmem((256, COLS), BF16),
            vmem((8, 16, DEPTH), BF16),
            vmem((128, DEPTH), BF16),
            vmem((2, 256, HALF), F32),
            vmem((2, 128, HALF), F32),
            vmem((2, 128, HALF), F32),
            vmem((2, 3, 32, HALF), F32),
            vmem((GROUPS, 128, FEATS), F32),
            vmem((GROUPS, 64, FEATS), F32),
            vmem((GROUPS, 64, FEATS), F32),
            vmem((GROUPS, 3, 16, FEATS), F32),
            vmem((2 + GROUPS, 128, 128), F32),
            vmem((2 + GROUPS, 120, 128), F32),
            vmem((2, 1024, 128), F32),
            vmem((FEATS, 512), BF16),
            vmem((64, 128), F32),
            dma((1,)),
            dma((2, 2)),
            dma((2, 1)),
            dma((2, PIECES)),
            dma((2, GROUPS * 2)),
            dma((2, 2 + GROUPS)),
            dma((2, 2 + GROUPS)),
            dma((2, 2 + GROUPS)),
            dma((2, 6)),
        ],
        compiler_params=pltpu.CompilerParams(
            collective_id=0, has_side_effects=True, vmem_limit_bytes=60 * 2**20
        ),
    )(train, target, proj, first, second, owners)


def solution(mesh):
    placed = (
        P("dp", "param"),
        P("dp", "param"),
        P("dp", "param"),
        P("param", "dp", None),
        P("param", "dp", None),
        P("param", None),
    )
    return jax.shard_map(
        per_device, mesh=mesh, in_specs=placed, out_specs=P(("dp", "param"), None), check_vma=False
    )
```

time: 538 us -> 110 us (0.20)
  waiting for transfers between devices: 442 us -> 0 us
  Pallas kernels: 0 us -> 109 us
  blocking collectives: 55.4 us -> 0 us
  matrix products: 14.3 us -> 0 us
  between operations: 13.5 us -> 0.01 us
  other arithmetic: 8.29 us -> 0 us
    all_gather x2 -> x0, waiting for transfers between devices: 442 us -> none  [the longest x1 251 us: per_device(): lax.all_gather(stacked, 'dp', axis=0, tiled=True)]
    pallas_call x0 -> x1, Pallas kernels: none -> 109 us  [per_device(): pl.pallas_call(kernel, out_shape=jax.ShapeDtypeStruct((4, 256), F32), in_...]
    all_gather x1 -> x0, blocking collectives: 29.5 us -> none  [side_by_side(): filled, at, done = (lax.all_gather(both, axis, axis=dim, tiled=True), 0, [])]
    all_to_all x2 -> x0, blocking collectives: 25.8 us -> none  [the longest x1 17.2 us: summed_on_arrival(): lax.all_to_all(blocks, axis, split_axis=0, concat_axis=0, tiled=True)]
    dot_general x2 -> x0, matrix products: 14.3 us -> none  [the longest x1 12.8 us: project(): lax.dot_general(grad_rows, projection, (((1,), (1,)), ((), ())), preferre...]
  transfers between devices with their start and end apart: 2 -> 0, of which waited for: 2 -> 0; matrix products, arithmetic and copies ran while one was open for 0% -> 0% of each run, Pallas kernels for 0% -> 0%
where the time goes in v2:
time: 110 us
  Pallas kernels  109 us (99%)
  local copies, waits for them, and re-layouts  1.28 us (1%)
    pallas_call x1, Pallas kernels, per_device(): pl.pallas_call(kernel, out_shape=jax.ShapeDtypeStruct((4, 256), F32), in_...  109 us

profile of v2, /device:TPU:0, one launch (start us, length us, event | category | flops | bytes accessed | tf_op | source)
XLA Modules:
  0.0 110.3 jit_solution(5081223266259565001)
XLA Ops:
  0.0 109.0 %shard_map.64 = f32[4,256]{1,0:T(4,128)} custom-call(bf16[64,16384]{1,0:T(8,128)(2,1)} %train.1, bf16[32,16384]{1,0:T(8,128)(2,1)} %target.1, bf16[128,16384]{1,0:T(8,128)(2,1)} %proj.1, f32[1,1,2048]{2,1,0:T(1,128)} %first.1, f32[1,1,2048]{2,1,0:T(1,128)} %second.1, s32[1,8]{1,0:T(1,128)} %owners.1), custom_call_target="tpu_custom_call" | custom-call | tf_op jit(solution)/shard_map/pallas_call | solution.py:383
  109.0 1.3 %copy.8 = f32[4,256]{1,0:T(4,128)} copy(f32[4,256]{1,0:T(4,128)} %shard_map.64) | data formatting | bytes 8192

commit v3 on v2

--- a/solution.py
+++ b/solution.py
@@ -15,7 +15,9 @@
 DEPTH = COLS // 2
 PIECES = 8
 GROUPS = 4
+LAST = GROUPS - 1
 FAR_FIRST = (2, 6, 5, 7, 1, 3, 4)
+XZ_FAR_FIRST = (10, 14, 13, 15, 9, 11, 12, 2, 6, 8, 5, 7, 1, 3, 4)
 
 
 def one_hot(rows, source_of, along=0):
@@ -34,7 +36,7 @@
     raw_rows, sorted_rows, all_targets, all_proj, columns_of, all_rows, all_first, all_second,
     target_lhs, mixed, lhs,
     target_part, target_from_core, target_by_y, target_from_y,
-    part, from_core, by_y, from_y, by_xz, from_xz, raw_unit, unit_cat, own_rows,
+    part, from_core, by_y, from_y, last_part, last_from_core, last_by_y, last_from_y, by_xz, from_xz, raw_unit, unit_cat, own_rows,
     load_sem, mom_sem, target_sem, proj_sem, row_sem, core_sem, y_sem, xz_sem, gather_sem,
 ):
     dp = lax.axis_index("dp")
@@ -179,7 +181,11 @@
         else:
             part[k] = part[k] + done
             away = pl.ds((1 - core) * 64, 64)
-            send(part.at[k, away], from_core.at[k], core_sem, 2 + k, core_peer)
+            if k == LAST:
+                last_part[...] = part[k, away].astype(BF16)
+                send(last_part, last_from_core, core_sem, 2 + k, core_peer)
+            else:
+                send(part.at[k, away], from_core.at[k], core_sem, 2 + k, core_peer)
 
     def add_core(g):
         if g < 2:
@@ -199,17 +205,34 @@
             other, device = y_peer(o)
             send(total.at[k, pl.ds(other * rows, rows)], arrived.at[k, o - 1], y_sem, g, device)
 
+    def add_core_last():
+        wait(last_from_core, core_sem.at[1, 5])
+        total = part[LAST, pl.ds(core * 64, 64)] + last_from_core[...].astype(F32)
+        by_y[LAST] = total
+        last_by_y[...] = total.astype(BF16)
+        for o in (2, 1, 3):
+            other, device = y_peer(o)
+            send(last_by_y.at[pl.ds(other * 16, 16)], last_from_y.at[o - 1], y_sem, 5, device)
+
     def add_y(g):
-        if g < 2:
+        if g == 5:
+            wait(last_from_y, y_sem.at[1, g])
+            total, k, rows = by_y, LAST, 16
+        elif g < 2:
             total, arrived, k, rows = target_by_y, target_from_y, g, 32
         else:
             total, arrived, k, rows = by_y, from_y, g - 2, 16
-        wait(arrived.at[k], y_sem.at[1, g])
-        done = total[k, pl.ds(y * rows, rows)] + arrived[k, 0] + arrived[k, 1] + arrived[k, 2]
+        done = total[k, pl.ds(y * rows, rows)]
+        if g < 5:
+            wait(arrived.at[k], y_sem.at[1, g])
+            done = done + arrived[k, 0] + arrived[k, 1] + arrived[k, 2]
+        else:
+            for o in range(3):
+                done = done + last_from_y[o].astype(F32)
         tiles = 128 // rows
         for s in range(tiles):
             by_xz[g, pl.ds(s, rows, stride=tiles), :] = done[:, s * 128 : (s + 1) * 128]
-        for o in range(1, 16):
+        for o in XZ_FAR_FIRST:
             other, device = xz_peer(o)
             send(by_xz.at[g, pl.ds(other * 8, 8)], from_xz.at[g, pl.ds(o * 8 - 8, 8)], xz_sem, g, device)
 
@@ -225,7 +248,7 @@
     def gather_xz(h):
         mine = raw_unit.at[h, pl.ds(spot * 8, 8)]
         raw_unit[h, pl.ds(spot * 8, 8)] = add_xz(h)
-        for o in range(1, 16):
+        for o in XZ_FAR_FIRST:
             send(mine, mine, gather_sem, h * 3, xz_peer(o)[1])
 
     def gather_y(h):
@@ -274,6 +297,27 @@
         f = add_xz(g)
         mean = jnp.sum(f * f, keepdims=True) / FEATS
         own_rows[(g - 2) * 8 : (g - 1) * 8] = f * lax.rsqrt(mean + 1e-06)
+
+    def sent():
+        wait(all_targets.at[pl.ds(0, 7)], target_sem.at[0, 0])
+        wait(all_first.at[pl.ds(0, 7)], mom_sem.at[0, 0])
+        wait(all_second.at[pl.ds(0, 7)], mom_sem.at[0, 1])
+        for i in range(PIECES):
+            wait(all_proj.at[i, pl.ds(0, 7)], proj_sem.at[0, i])
+        for h in range(2):
+            wait(target_from_core.at[h], core_sem.at[0, h])
+            wait(target_from_y.at[h], y_sem.at[0, h])
+            wait(from_xz.at[h], xz_sem.at[0, h])
+            wait(raw_unit.at[h, pl.ds(0, 120)], gather_sem.at[0, h * 3])
+            wait(raw_unit.at[h, pl.ds(0, 384)], gather_sem.at[0, h * 3 + 1])
+            wait(raw_unit.at[h, pl.ds(0, 512)], gather_sem.at[0, h * 3 + 2])
+        for at in range(GROUPS * 2):
+            wait(all_rows.at[at, pl.ds(0, 7)], row_sem.at[0, at])
+        for k in range(GROUPS):
+            wait(last_from_core if k == LAST else from_core.at[k], core_sem.at[0, 2 + k])
+            wait(last_from_y if k == LAST else from_y.at[k], y_sem.at[0, 2 + k])
+            if k != LAST:
+                wait(from_xz.at[2 + k], xz_sem.at[0, 2 + k])
 
     send_targets()
     send_proj(0)
@@ -337,14 +381,15 @@
     add_core(4)
     multiply(3, 0)
     multiply(3, 1)
+    add_core_last()
     gather_core(1)
-    add_core(5)
+    add_y(4)
     train_row(2)
-    add_y(4)
     train_row(3)
     arrange()
+    add_y(5)
+    sent()
     train_row(4)
-    add_y(5)
     train_row(5)
 
     rows = jnp.concatenate([own_rows[pl.ds(s, 8, stride=8), :] for s in range(8)], axis=1)
@@ -356,24 +401,7 @@
     scaled = product[0:8, 0:256] + (product[8:16, 0:256] + product[0:8, 256:512])
     out[...] = scaled[0:4] / math.sqrt(FEATS)
 
-    wait(all_targets.at[pl.ds(0, 7)], target_sem.at[0, 0])
-    wait(all_first.at[pl.ds(0, 7)], mom_sem.at[0, 0])
-    wait(all_second.at[pl.ds(0, 7)], mom_sem.at[0, 1])
-    for i in range(PIECES):
-        wait(all_proj.at[i, pl.ds(0, 7)], proj_sem.at[0, i])
-    for h in range(2):
-        wait(target_from_core.at[h], core_sem.at[0, h])
-        wait(target_from_y.at[h], y_sem.at[0, h])
-        wait(from_xz.at[h], xz_sem.at[0, h])
-        wait(raw_unit.at[h, pl.ds(0, 120)], gather_sem.at[0, h * 3])
-        wait(raw_unit.at[h, pl.ds(0, 384)], gather_sem.at[0, h * 3 + 1])
-        wait(raw_unit.at[h, pl.ds(0, 512)], gather_sem.at[0, h * 3 + 2])
-    for at in range(GROUPS * 2):
-        wait(all_rows.at[at, pl.ds(0, 7)], row_sem.at[0, at])
-    for k in range(GROUPS):
-        wait(from_core.at[k], core_sem.at[0, 2 + k])
-        wait(from_y.at[k], y_sem.at[0, 2 + k])
-        wait(from_xz.at[2 + k], xz_sem.at[0, 2 + k])
+    wait(from_xz.at[5], xz_sem.at[0, 5])
 
 
 def per_device(train, target, proj, first, second, owners):
@@ -402,9 +430,13 @@
             vmem((2, 128, HALF), F32),
             vmem((2, 3, 32, HALF), F32),
             vmem((GROUPS, 128, FEATS), F32),
+            vmem((LAST, 64, FEATS), F32),
             vmem((GROUPS, 64, FEATS), F32),
-            vmem((GROUPS, 64, FEATS), F32),
-            vmem((GROUPS, 3, 16, FEATS), F32),
+            vmem((LAST, 3, 16, FEATS), F32),
+            vmem((64, FEATS), BF16),
+            vmem((64, FEATS), BF16),
+            vmem((64, FEATS), BF16),
+            vmem((3, 16, FEATS), BF16),
             vmem((2 + GROUPS, 128, 128), F32),
             vmem((2 + GROUPS, 120, 128), F32),
             vmem((2, 1024, 128), F32),

time: 110 us -> 108 us (0.982); the launches traced: 110 us -> 107 us
  Pallas kernels: 109 us -> 106 us
    pallas_call x1, Pallas kernels: 109 us -> 106 us  [per_device(): pl.pallas_call(kernel, out_shape=jax.ShapeDtypeStruct((4, 256), F32), in_...]
where the time goes in v3:
time: 108 us; the launch traced here: 107 us
  Pallas kernels  106 us (98%)
  local copies, waits for them, and re-layouts  1.28 us (1%)
    pallas_call x1, Pallas kernels, per_device(): pl.pallas_call(kernel, out_shape=jax.ShapeDtypeStruct((4, 256), F32), in_...  106 us

profile of v3, /device:TPU:0, one launch (start us, length us, event | category | flops | bytes accessed | tf_op | source)
XLA Modules:
  0.0 107.0 jit_solution(7276890935657779646)
XLA Ops:
  0.0 105.8 %shard_map.64 = f32[4,256]{1,0:T(4,128)} custom-call(bf16[64,16384]{1,0:T(8,128)(2,1)} %train.1, bf16[32,16384]{1,0:T(8,128)(2,1)} %target.1, bf16[128,16384]{1,0:T(8,128)(2,1)} %proj.1, f32[1,1,2048]{2,1,0:T(1,128)} %first.1, f32[1,1,2048]{2,1,0:T(1,128)} %second.1, s32[1,8]{1,0:T(1,128)} %owners.1), custom_call_target="tpu_custom_call" | custom-call | tf_op jit(solution)/shard_map/pallas_call | solution.py:411
  105.8 1.3 %copy.8 = f32[4,256]{1,0:T(4,128)} copy(f32[4,256]{1,0:T(4,128)} %shard_map.64) | data formatting | bytes 8192

commit v4 on v3

--- a/solution.py
+++ b/solution.py
@@ -13,6 +13,7 @@
 FEATS = 1024
 HALF = 512
 DEPTH = COLS // 2
+SHORT = 512
 PIECES = 8
 GROUPS = 4
 LAST = GROUPS - 1
@@ -31,13 +32,14 @@
 
 
 def kernel(
-    train, target, proj, first, second, owners,
+    train, target, proj, first, second, owner_map,
     out,
-    raw_rows, sorted_rows, all_targets, all_proj, columns_of, all_rows, all_first, all_second,
+    owners, raw_rows, sorted_rows, all_targets, all_proj, columns_of, all_rows, last_long, last_short, all_first, all_second,
     target_lhs, mixed, lhs,
     target_part, target_from_core, target_by_y, target_from_y,
     part, from_core, by_y, from_y, last_part, last_from_core, last_by_y, last_from_y, by_xz, from_xz, raw_unit, unit_cat, own_rows,
     load_sem, mom_sem, target_sem, proj_sem, row_sem, core_sem, y_sem, xz_sem, gather_sem,
+    last_core_sem, last_y_sem,
 ):
     dp = lax.axis_index("dp")
     param = lax.axis_index("param")
@@ -72,11 +74,12 @@
     def columns(owner):
         return pl.ds(owner * COLS, COLS)
 
-    keep(train, raw_rows, load_sem.at[0])
     barrier = pltpu.get_barrier_semaphore()
     peers = [xz_peer(o)[1] for o in range(1, 16)] + [core_peer] + [y_peer(o)[1] for o in range(1, 4)]
     for device in peers:
         pl.semaphore_signal(barrier, inc=1, device_id=device, device_id_type=MESH)
+    keep(train, raw_rows, load_sem.at[0])
+    keep(owner_map, owners, load_sem.at[1])
     pl.semaphore_wait(barrier, len(peers))
 
     def send_targets():
@@ -100,16 +103,22 @@
         keep(first.at[0], all_first.at[dp], mom_sem.at[1, 0])
         keep(second.at[0], all_second.at[dp], mom_sem.at[1, 1])
 
+    def piece_of(k, half):
+        if k < LAST:
+            return half * DEPTH, DEPTH, all_rows.at[k * 2 + half]
+        return (COLS - SHORT, SHORT, last_short) if half else (0, COLS - SHORT, last_long)
+
     def send_rows(k, half):
         rows, at = pl.ds(k * 16, 16), k * 2 + half
+        start, width, there = piece_of(k, half)
 
         def some(owner):
-            return sorted_rows.at[rows, pl.ds(owner * COLS + half * DEPTH, DEPTH)]
+            return sorted_rows.at[rows, pl.ds(owner * COLS + start, width)]
 
         for o in FAR_FIRST:
             other, device = dp_peer(o)
-            send(some(other), all_rows.at[at, dp], row_sem, at, device)
-        keep(some(dp), all_rows.at[at, dp], row_sem.at[1, at])
+            send(some(other), there.at[dp], row_sem, at, device)
+        keep(some(dp), there.at[dp], row_sem.at[1, at])
 
     def sort_rows():
         wait(raw_rows, load_sem.at[0])
@@ -156,36 +165,37 @@
 
     def multiply(k, half):
         at = k * 2 + half
-        wait(all_rows.at[at], row_sem.at[1, at])
+        start, width, here = piece_of(k, half)
+        wait(here, row_sem.at[1, at])
 
         @pl.loop(0, 8)
         def _(s):
-            for t in range(2):
+            for t in range(width // 512):
                 cols = slice(t * 512, (t + 1) * 512)
-                own = slice(half * DEPTH + t * 512, half * DEPTH + (t + 1) * 512)
-                g = all_rows[at, s, :, cols].astype(F32)
+                own = slice(start + t * 512, start + (t + 1) * 512)
+                g = here[s, :, cols].astype(F32)
                 upper = first_row[:, own] + 0.1 * g
                 lower = jnp.sqrt(second_row[:, own] + 0.001 * g * g) + 1e-08
                 mixed[s, :, cols] = (upper / lower).astype(BF16)
 
-        for t in range(2):
+        for t in range(width // 512):
             cols = slice(t * 512, (t + 1) * 512)
             lhs[:, cols] = jnp.dot(
                 regroup, mixed[:, :, cols].reshape(128, 512), preferred_element_type=F32
             ).astype(BF16)
-        done = jnp.dot(
-            lhs[...], columns_of[half * DEPTH : (half + 1) * DEPTH], preferred_element_type=F32
-        )
-        if half == 0:
-            part[k] = done
-        else:
-            part[k] = part[k] + done
-            away = pl.ds((1 - core) * 64, 64)
-            if k == LAST:
-                last_part[...] = part[k, away].astype(BF16)
-                send(last_part, last_from_core, core_sem, 2 + k, core_peer)
-            else:
-                send(part.at[k, away], from_core.at[k], core_sem, 2 + k, core_peer)
+        away = pl.ds((1 - core) * 64, 64)
+        for h in range(2):
+            cols = slice(h * HALF, (h + 1) * HALF)
+            done = jnp.dot(
+                lhs[:, 0:width], columns_of[start : start + width, cols],
+                preferred_element_type=F32,
+            )
+            part[k, :, cols] = done if half == 0 else part[k, :, cols] + done
+            if half == 1 and k == LAST:
+                last_part[h] = part[k, away, cols].astype(BF16)
+                send(last_part.at[h], last_from_core.at[h], last_core_sem, h, core_peer)
+        if half == 1 and k < LAST:
+            send(part.at[k, away], from_core.at[k], core_sem, 2 + k, core_peer)
 
     def add_core(g):
         if g < 2:
@@ -205,19 +215,22 @@
             other, device = y_peer(o)
             send(total.at[k, pl.ds(other * rows, rows)], arrived.at[k, o - 1], y_sem, g, device)
 
-    def add_core_last():
-        wait(last_from_core, core_sem.at[1, 5])
-        total = part[LAST, pl.ds(core * 64, 64)] + last_from_core[...].astype(F32)
-        by_y[LAST] = total
-        last_by_y[...] = total.astype(BF16)
+    def add_core_last(h):
+        cols = slice(h * HALF, (h + 1) * HALF)
+        wait(last_from_core.at[h], last_core_sem.at[1, h])
+        total = part[LAST, pl.ds(core * 64, 64), cols] + last_from_core[h].astype(F32)
+        by_y[LAST, :, cols] = total
+        last_by_y[h] = total.astype(BF16)
         for o in (2, 1, 3):
             other, device = y_peer(o)
-            send(last_by_y.at[pl.ds(other * 16, 16)], last_from_y.at[o - 1], y_sem, 5, device)
+            rows = pl.ds(other * 16, 16)
+            send(last_by_y.at[h, rows], last_from_y.at[h, o - 1], last_y_sem, h, device)
 
     def add_y(g):
         if g == 5:
-            wait(last_from_y, y_sem.at[1, g])
             total, k, rows = by_y, LAST, 16
+            for h in range(2):
+                wait(last_from_y.at[h], last_y_sem.at[1, h])
         elif g < 2:
             total, arrived, k, rows = target_by_y, target_from_y, g, 32
         else:
@@ -228,7 +241,8 @@
             done = done + arrived[k, 0] + arrived[k, 1] + arrived[k, 2]
         else:
             for o in range(3):
-                done = done + last_from_y[o].astype(F32)
+                both = [last_from_y[h, o].astype(F32) for h in range(2)]
+                done = done + jnp.concatenate(both, axis=1)
         tiles = 128 // rows
         for s in range(tiles):
             by_xz[g, pl.ds(s, rows, stride=tiles), :] = done[:, s * 128 : (s + 1) * 128]
@@ -311,13 +325,16 @@
             wait(raw_unit.at[h, pl.ds(0, 120)], gather_sem.at[0, h * 3])
             wait(raw_unit.at[h, pl.ds(0, 384)], gather_sem.at[0, h * 3 + 1])
             wait(raw_unit.at[h, pl.ds(0, 512)], gather_sem.at[0, h * 3 + 2])
-        for at in range(GROUPS * 2):
-            wait(all_rows.at[at, pl.ds(0, 7)], row_sem.at[0, at])
-        for k in range(GROUPS):
-            wait(last_from_core if k == LAST else from_core.at[k], core_sem.at[0, 2 + k])
-            wait(last_from_y if k == LAST else from_y.at[k], y_sem.at[0, 2 + k])
-            if k != LAST:
-                wait(from_xz.at[2 + k], xz_sem.at[0, 2 + k])
+        for h in range(2):
+            wait(piece_of(LAST, h)[2].at[pl.ds(0, 7)], row_sem.at[0, LAST * 2 + h])
+            wait(last_from_core.at[h], last_core_sem.at[0, h])
+            wait(last_from_y.at[h], last_y_sem.at[0, h])
+        for k in range(LAST):
+            for h in range(2):
+                wait(all_rows.at[k * 2 + h, pl.ds(0, 7)], row_sem.at[0, k * 2 + h])
+            wait(from_core.at[k], core_sem.at[0, 2 + k])
+            wait(from_y.at[k], y_sem.at[0, 2 + k])
+            wait(from_xz.at[2 + k], xz_sem.at[0, 2 + k])
 
     send_targets()
     send_proj(0)
@@ -333,6 +350,7 @@
     send_proj(4)
     wait(all_first, mom_sem.at[1, 0])
     wait(all_second, mom_sem.at[1, 1])
+    pltpu.make_async_copy(owner_map, owners, load_sem.at[1]).wait()
     owner = owners[0, dp]
     first_row = 0.9 * all_first[owner]
     second_row = 0.999 * all_second[owner]
@@ -381,7 +399,8 @@
     add_core(4)
     multiply(3, 0)
     multiply(3, 1)
-    add_core_last()
+    add_core_last(0)
+    add_core_last(1)
     gather_core(1)
     add_y(4)
     train_row(2)
@@ -411,20 +430,23 @@
     return pl.pallas_call(
         kernel,
         out_shape=jax.ShapeDtypeStruct((4, 256), F32),
-        in_specs=[anywhere] * 5 + [pl.BlockSpec(memory_space=pltpu.SMEM)],
+        in_specs=[anywhere] * 6,
         out_specs=pl.BlockSpec(memory_space=pltpu.VMEM),
         scratch_shapes=[
+            pltpu.SMEM((1, 8), jnp.int32),
             vmem((64, 16384), BF16),
             vmem((64, 16384), BF16),
             vmem((8, 32, COLS), BF16),
             vmem((PIECES, 8, 16, COLS), BF16),
             vmem((COLS, FEATS), BF16),
-            vmem((GROUPS * 2, 8, 16, DEPTH), BF16),
+            vmem((LAST * 2, 8, 16, DEPTH), BF16),
+            vmem((8, 16, COLS - SHORT), BF16),
+            vmem((8, 16, SHORT), BF16),
             vmem((8, 1, COLS), F32),
             vmem((8, 1, COLS), F32),
             vmem((256, COLS), BF16),
-            vmem((8, 16, DEPTH), BF16),
-            vmem((128, DEPTH), BF16),
+            vmem((8, 16, COLS - SHORT), BF16),
+            vmem((128, COLS - SHORT), BF16),
             vmem((2, 256, HALF), F32),
             vmem((2, 128, HALF), F32),
             vmem((2, 128, HALF), F32),
@@ -433,24 +455,26 @@
             vmem((LAST, 64, FEATS), F32),
             vmem((GROUPS, 64, FEATS), F32),
             vmem((LAST, 3, 16, FEATS), F32),
-            vmem((64, FEATS), BF16),
-            vmem((64, FEATS), BF16),
-            vmem((64, FEATS), BF16),
-            vmem((3, 16, FEATS), BF16),
+            vmem((2, 64, HALF), BF16),
+            vmem((2, 64, HALF), BF16),
+            vmem((2, 64, HALF), BF16),
+            vmem((2, 3, 16, HALF), BF16),
             vmem((2 + GROUPS, 128, 128), F32),
             vmem((2 + GROUPS, 120, 128), F32),
             vmem((2, 1024, 128), F32),
             vmem((FEATS, 512), BF16),
             vmem((64, 128), F32),
-            dma((1,)),
+            dma((2,)),
             dma((2, 2)),
             dma((2, 1)),
             dma((2, PIECES)),
             dma((2, GROUPS * 2)),
-            dma((2, 2 + GROUPS)),
-            dma((2, 2 + GROUPS)),
+            dma((2, 2 + LAST)),
+            dma((2, 2 + LAST)),
             dma((2, 2 + GROUPS)),
             dma((2, 6)),
+            dma((2, 2)),
+            dma((2, 2)),
         ],
         compiler_params=pltpu.CompilerParams(
             collective_id=0, has_side_effects=True, vmem_limit_bytes=60 * 2**20

time: 108 us -> 107 us (level)
  no operation moved by 1% of the time
where the time goes in v4:
time: 107 us
  Pallas kernels  105 us (98%)
  local copies, waits for them, and re-layouts  1.28 us (1%)
    pallas_call x1, Pallas kernels, per_device(): pl.pallas_call(kernel, out_shape=jax.ShapeDtypeStruct((4, 256), F32), in_...  105 us

profile of v4, /device:TPU:0, one launch (start us, length us, event | category | flops | bytes accessed | tf_op | source)
XLA Modules:
  0.0 106.8 jit_solution(8380983723836658995)
XLA Ops:
  0.0 105.5 %shard_map.64 = f32[4,256]{1,0:T(4,128)} custom-call(bf16[64,16384]{1,0:T(8,128)(2,1)} %train.1, bf16[32,16384]{1,0:T(8,128)(2,1)} %target.1, bf16[128,16384]{1,0:T(8,128)(2,1)} %proj.1, f32[1,1,2048]{2,1,0:T(1,128)} %first.1, f32[1,1,2048]{2,1,0:T(1,128)} %second.1, s32[1,8]{1,0:T(1,128)} %owner_map.1), custom_call_target="tpu_custom_call" | custom-call | tf_op jit(solution)/shard_map/pallas_call | solution.py:430
  105.5 1.3 %copy.8 = f32[4,256]{1,0:T(4,128)} copy(f32[4,256]{1,0:T(4,128)} %shard_map.64) | data formatting | bytes 8192

commit v5 on v4

--- a/solution.py
+++ b/solution.py
@@ -477,9 +477,9 @@
             dma((2, 2)),
         ],
         compiler_params=pltpu.CompilerParams(
-            collective_id=0, has_side_effects=True, vmem_limit_bytes=60 * 2**20
+            collective_id=0, has_side_effects=True, vmem_limit_bytes=40 * 2**20
         ),
-    )(train, target, proj, first, second, owners)
+    )(*(pltpu.with_memory_space_constraint(a, pltpu.HBM) for a in (train, target, proj, first, second, owners)))
 
 
 def solution(mesh):

time: 107 us -> 106 us (level)
  no operation moved by 1% of the time
where the time goes in v5:
time: 106 us; the launch traced here: 105 us
  Pallas kernels  105 us (99%)
    pallas_call x1, Pallas kernels, per_device(): pl.pallas_call(kernel, out_shape=jax.ShapeDtypeStruct((4, 256), F32), in_...  105 us

profile of v5, /device:TPU:0, one launch (start us, length us, event | category | flops | bytes accessed | tf_op | source)
XLA Modules:
  0.0 105.5 jit_solution(17276847109689080315)
XLA Ops:
  0.0 104.9 %shard_map.64 = f32[4,256]{1,0:T(4,128)S(1)} custom-call(bf16[64,16384]{1,0:T(8,128)(2,1)} %train.1, bf16[32,16384]{1,0:T(8,128)(2,1)} %target.1, bf16[128,16384]{1,0:T(8,128)(2,1)} %proj.1, f32[1,1,2048]{2,1,0:T(1,128)} %first.1, f32[1,1,2048]{2,1,0:T(1,128)} %second.1, s32[1,8]{1,0:T(1,128)} %owner_map.1), custom_call_target="tpu_custom_call" | custom-call | tf_op jit(solution)/shard_map/pallas_call | solution.py:430
  104.9 0.6 copy.8

commit v6 on v5

--- a/solution.py
+++ b/solution.py
@@ -390,23 +390,23 @@
     send_rows(3, 0)
     send_rows(3, 1)
     add_core(3)
-    add_y(2)
     gather_core(0)
     multiply(2, 0)
     multiply(2, 1)
     gather_y(1)
-    add_y(3)
     add_core(4)
     multiply(3, 0)
     multiply(3, 1)
     add_core_last(0)
     add_core_last(1)
+    add_y(2)
+    add_y(3)
     gather_core(1)
     add_y(4)
+    arrange()
+    add_y(5)
     train_row(2)
     train_row(3)
-    arrange()
-    add_y(5)
     sent()
     train_row(4)
     train_row(5)

time: 106 us -> 106 us (level)
  no operation moved by 1% of the time
where the time goes in v6:
time: 106 us; the launch traced here: 105 us
  Pallas kernels  104 us (98%)
    pallas_call x1, Pallas kernels, per_device(): pl.pallas_call(kernel, out_shape=jax.ShapeDtypeStruct((4, 256), F32), in_...  104 us

profile of v6, /device:TPU:0, one launch (start us, length us, event | category | flops | bytes accessed | tf_op | source)
XLA Modules:
  0.0 105.0 jit_solution(17668465231618899743)
XLA Ops:
  0.0 104.4 %shard_map.64 = f32[4,256]{1,0:T(4,128)S(1)} custom-call(bf16[64,16384]{1,0:T(8,128)(2,1)} %train.1, bf16[32,16384]{1,0:T(8,128)(2,1)} %target.1, bf16[128,16384]{1,0:T(8,128)(2,1)} %proj.1, f32[1,1,2048]{2,1,0:T(1,128)} %first.1, f32[1,1,2048]{2,1,0:T(1,128)} %second.1, s32[1,8]{1,0:T(1,128)} %owner_map.1), custom_call_target="tpu_custom_call" | custom-call | tf_op jit(solution)/shard_map/pallas_call | solution.py:430
  104.4 0.6 copy.8

commit v7 on v6

--- a/solution.py
+++ b/solution.py
@@ -75,7 +75,7 @@
         return pl.ds(owner * COLS, COLS)
 
     barrier = pltpu.get_barrier_semaphore()
-    peers = [xz_peer(o)[1] for o in range(1, 16)] + [core_peer] + [y_peer(o)[1] for o in range(1, 4)]
+    peers = [xz_peer(o)[1] for o in XZ_FAR_FIRST] + [y_peer(o)[1] for o in (2, 1, 3)] + [core_peer]
     for device in peers:
         pl.semaphore_signal(barrier, inc=1, device_id=device, device_id_type=MESH)
     keep(train, raw_rows, load_sem.at[0])

time: 106 us -> 106 us (level)
  no operation moved by 1% of the time
where the time goes in v7:
time: 106 us; the launch traced here: 105 us
  Pallas kernels  104 us (98%)
    pallas_call x1, Pallas kernels, per_device(): pl.pallas_call(kernel, out_shape=jax.ShapeDtypeStruct((4, 256), F32), in_...  104 us

profile of v7, /device:TPU:0, one launch (start us, length us, event | category | flops | bytes accessed | tf_op | source)
XLA Modules:
  0.0 104.9 jit_solution(4546013984222273961)
XLA Ops:
  0.0 104.3 %shard_map.64 = f32[4,256]{1,0:T(4,128)S(1)} custom-call(bf16[64,16384]{1,0:T(8,128)(2,1)} %train.1, bf16[32,16384]{1,0:T(8,128)(2,1)} %target.1, bf16[128,16384]{1,0:T(8,128)(2,1)} %proj.1, f32[1,1,2048]{2,1,0:T(1,128)} %first.1, f32[1,1,2048]{2,1,0:T(1,128)} %second.1, s32[1,8]{1,0:T(1,128)} %owner_map.1), custom_call_target="tpu_custom_call" | custom-call | tf_op jit(solution)/shard_map/pallas_call | solution.py:430
  104.3 0.6 copy.8
